TPU v7x, 256 devices: a whole 4x4x8 slice. The times are simulated.
256 devices in a mesh: tok: 64 (over y, z, core), grp: 4 (over x).
Axes of the slice: x: 4, y: 4, z: 8, core: 2. Of those that a mesh axis runs over, the one named last changes fastest.
Arguments:
- tokens: bfloat16 [98304, 1024], P(('tok', 'grp')), may hold values from -6 to 6
- norm_gain: float32 [1024], replicated, may hold values from 0.25 to 1.75
- input_weight: bfloat16 [1024, 3072], P('tok', 'grp')
- output_weight: bfloat16 [1024, 1024], P('tok', 'grp'), may hold values from -2 to 2
- segment_ids: int32 [98304], replicated, may hold values from 0 to 191, never falling along the last dimension, each value on 1 to 1024 neighbouring positions
- page_owner: int32 [24576, 1], P(('tok', 'grp')), may hold values from 0 to 63; in each aligned block of 96 rows (0 to 95, 96 to 191, ...) at most 3 rows name the same one
Outputs:
- attended: bfloat16 [98304, 1024], P(('tok', 'grp'))
- cache_pages: bfloat16 [49152, 8192], P(('tok', 'grp'))
Inputs may be any that keep to these rules, and one draw needn't show every extreme that they name: `segment_ids`: segment ids never fall along the pack; every id occurs on 1 to 1024 consecutive tokens, and some document has exactly 1024 tokens. `page_owner`: within the 96 pages of one device no owner is named more than 3 times, and in some device one owner is named exactly 3 times.
All inputs are finite; a program needn't handle non-finite values.
Results may differ from a plain program's by a relative error of at most 0.0089.
Values may be sent and summed in bfloat16 or wider, within the bound.
A program may use at most 128 MiB of HBM per device.

v0:
```python
import jax
import jax.numpy as jnp
from jax import lax
from jax.sharding import PartitionSpec as P

H = 16
SPAN = 1024
PAGE = 4
NEG_FILL = -1e30
ROPE_BASE = 160000.0
EPSILON = 1e-05


def shifted(value, axis, steps):
    count = lax.axis_size(axis)
    initial, last = (max(0, -steps), min(count, count - steps))
    return lax.ppermute(value, axis, [(source, source + steps) for source in range(initial, last)])


def layer_norm(tokens, norm_gain):
    values = tokens.astype(jnp.float32)
    center = jnp.mean(values, axis=-1, keepdims=True)
    spread = jnp.mean(jnp.square(values - center), axis=-1, keepdims=True)
    return ((values - center) * lax.rsqrt(spread + EPSILON) * norm_gain).astype(jnp.bfloat16)


def rotate(block_part, positions, head_count):
    row_count = block_part.shape[0]
    head_dim = block_part.shape[1] // head_count
    half_dim = head_dim // 2
    shaped = block_part.reshape(row_count, head_count, head_dim)
    inverse = 1.0 / ROPE_BASE ** (jnp.arange(half_dim, dtype=jnp.float32) * 2.0 / head_dim)
    angles = positions.astype(jnp.float32)[:, None] * inverse[None, :]
    cosine = jnp.concatenate([jnp.cos(angles), jnp.cos(angles)], axis=1)[:, None, :]
    sine_table = jnp.concatenate([jnp.sin(angles), jnp.sin(angles)], axis=1)[:, None, :]
    turned = jnp.concatenate([-shaped[..., half_dim:], shaped[..., :half_dim]], axis=-1)
    return (
        (shaped * cosine + turned * sine_table)
        .reshape(row_count, head_count * head_dim)
        .astype(jnp.bfloat16)
    )


def positions_of(segment_ids, own_ids, first_row):
    starts = jnp.searchsorted(segment_ids, own_ids, side="left")
    return first_row + jnp.arange(own_ids.shape[0], dtype=jnp.int32) - starts


def pair_scores(query_pair, key_pair, score_scale):
    return (
        jnp.einsum("tnd,snd->nts", query_pair, key_pair, preferred_element_type=jnp.float32)
        * score_scale
    )


def attend_pairs(queries, key_window, value_window, allowed, head_count):
    row_count = queries.shape[0]
    window_len = key_window.shape[0]
    head_dim = queries.shape[1] // head_count
    pair_count = head_count // 2
    score_scale = head_dim ** (-0.5)
    query_stack = jnp.transpose(queries.reshape(row_count, pair_count, 2, head_dim), (1, 0, 2, 3))
    key_stack = jnp.transpose(key_window.reshape(window_len, pair_count, 2, head_dim), (1, 0, 2, 3))
    value_stack = jnp.transpose(
        value_window.reshape(window_len, pair_count, 2, head_dim), (1, 0, 2, 3)
    )

    def one_pair(operands):
        query_pair, key_pair, value_pair = operands
        scores = jnp.where(allowed[None], pair_scores(query_pair, key_pair, score_scale), NEG_FILL)
        row_peak = jnp.max(scores, axis=-1, keepdims=True)
        exponent = jnp.exp(scores - row_peak)
        row_total = jnp.sum(exponent, axis=-1)
        weights = exponent.astype(jnp.bfloat16)
        mixed_rows = jnp.einsum(
            "nts,snd->tnd", weights, value_pair, preferred_element_type=jnp.float32
        )
        return mixed_rows / jnp.transpose(row_total)[:, :, None]

    mixed_stack = lax.map(one_pair, (query_stack, key_stack, value_stack))
    return (
        jnp.transpose(mixed_stack, (1, 0, 2, 3))
        .reshape(row_count, head_count * head_dim)
        .astype(jnp.bfloat16)
    )


def per_device(tokens, norm_gain, input_weight, output_weight, segment_ids, page_owner):
    row_count = tokens.shape[0]
    model_width = tokens.shape[1]
    device = lax.axis_index(("tok", "grp"))
    first_row = device * row_count
    normed = layer_norm(tokens, norm_gain)
    input_cols, output_cols = (
        lax.all_gather(input_weight, "grp", axis=1, tiled=True),
        lax.all_gather(output_weight, "grp", axis=1, tiled=True),
    )
    section = normed
    joined = jnp.dot(
        section,
        lax.all_gather(input_cols, "tok", axis=0, tiled=True),
        preferred_element_type=jnp.float32,
    )
    own_ids = lax.dynamic_slice_in_dim(segment_ids, first_row, row_count, 0)
    positions = positions_of(segment_ids, own_ids, first_row)
    queries = rotate(joined[:, :model_width], positions, H)
    key_rows = rotate(joined[:, model_width : 2 * model_width], positions, H)
    value_rows = joined[:, 2 * model_width :].astype(jnp.bfloat16)
    paired = jnp.stack([key_rows, value_rows])
    reach_blocks = (SPAN + row_count - 2) // row_count
    window_len = (2 * reach_blocks + 1) * row_count
    earlier = [shifted(paired, ("tok", "grp"), distance) for distance in range(reach_blocks, 0, -1)]
    later_blocks = [
        shifted(paired, ("tok", "grp"), -distance) for distance in range(1, reach_blocks + 1)
    ]
    window = jnp.concatenate(earlier + [paired] + later_blocks, axis=1)
    filler = jnp.full((reach_blocks * row_count,), -1, jnp.int32)
    padded_ids = jnp.concatenate([filler, segment_ids, filler])
    window_ids = lax.dynamic_slice_in_dim(padded_ids, first_row, window_len, 0)
    allowed = own_ids[:, None] == window_ids[None, :]
    mixed_rows = attend_pairs(queries, window[0], window[1], allowed, H)
    section = mixed_rows
    attended = jnp.dot(
        section,
        lax.all_gather(output_cols, "tok", axis=0, tiled=True),
        preferred_element_type=jnp.float32,
    ).astype(jnp.bfloat16)
    page_rows = jnp.concatenate([key_rows, value_rows], axis=1).reshape(
        row_count // PAGE, 2 * PAGE * model_width
    )
    owners = page_owner[:, 0]
    page_count = owners.shape[0]
    earlier_mask = jnp.arange(page_count)[:, None] > jnp.arange(page_count)[None, :]
    page_ranks = jnp.sum(
        ((owners[:, None] == owners[None, :]) & earlier_mask).astype(jnp.int32), axis=1
    )
    peer_count = lax.axis_size("tok")
    capacity = max(2, (2 * page_count + peer_count - 1) // peer_count)
    send_slots = jnp.zeros((peer_count * capacity, page_rows.shape[1]), jnp.bfloat16)
    send_slots = send_slots.at[owners * capacity + page_ranks].set(page_rows)
    cache_pages = lax.all_to_all(send_slots, "tok", split_axis=0, concat_axis=0, tiled=True)
    return (attended, cache_pages)


def solution(mesh):
    placed = (
        P(("tok", "grp"), None),
        P(),
        P("tok", "grp"),
        P("tok", "grp"),
        P(),
        P(("tok", "grp"), None),
    )
    return jax.shard_map(
        per_device,
        mesh=mesh,
        in_specs=placed,
        out_specs=(P(("tok", "grp"), None), P(("tok", "grp"), None)),
        check_vma=False,
    )
```

profile of v0, /device:TPU:1, one launch (start us, length us, event | category | flops | bytes accessed | tf_op | source)
XLA Modules:
  0.0 458.8 jit_solution(4806925202576879841)
XLA Ops:
  7.2 12.0 %all_gather.12 = bf16[16,3072]{1,0:T(8,128)(2,1)} all-gather(bf16[16,768]{1,0:T(8,128)(2,1)} %param.12), channel_id=1, replica_groups=mesh['tok'=64,'grp'=4] {'grp'}, dimensions={1}, use_global_device_ids=true | all-gather | bytes 122880 | tf_op jit(solution)/shard_map/all_gather | solution.py:95
  20.1 64.1 %while.36 = (s32[]{:T(128)}, u32[384]{0:T(512)S(1)}, u32[384]{0:T(512)S(1)}, s32[98304]{0:T(1024)}, s32[384]{0:T(512)S(1)}, /*index=5*/s32[]{:T(128)}, s32[]{:T(128)}, s32[]{}) while((s32[]{:T(128)}, u32[384]{0:T(512)S(1)}, u32[384]{0:T(512)S(1)}, s32[98304]{0:T(1024)}, s32[384]{0:T(512)S(1)}, /*index=5*/s32[]{:T(128)}, s32[]{:T(128)}, ...), condition=%wide.region_3.4_spmd.clone, body=%wide.region_2.3_spmd.clone.sunk | while | flops 7940 | bytes 31085 | solution.py:45
  20.1 3.7 gather_fusion
  23.8 3.7 gather_fusion
  27.6 3.7 gather_fusion
  31.4 3.7 gather_fusion
  35.2 3.7 gather_fusion
  38.9 3.7 gather_fusion
  42.7 3.7 gather_fusion
  46.5 3.7 gather_fusion
  50.2 3.7 gather_fusion
  54.0 3.7 gather_fusion
  57.8 3.7 gather_fusion
  61.5 3.7 gather_fusion
  65.3 3.7 gather_fusion
  69.1 3.7 gather_fusion
  72.8 3.8 gather_fusion
  76.7 3.7 gather_fusion
  80.5 3.7 gather_fusion
  88.8 16.0 %all-gather.3.cloned.1.call-done = bf16[1024,3072]{1,0:T(8,128)(2,1)} async-done(((bf16[16,3072]{1,0:T(8,128)(2,1)}), bf16[1024,3072]{1,0:T(8,128)(2,1)}) %all-gather.3.cloned.1.call-update) | async-done | bytes 6291472 | tf_op jit(solution)/shard_map/all_gather | solution.py:101
  104.8 5.1 %fusion.38 = f32[384,3072]{1,0:T(8,128)S(1)} fusion(bf16[1024,3072]{1,0:T(8,128)(2,1)} %all-gather.3.cloned.1.call-done, bf16[384,1024]{1,0:T(8,128)(2,1)} %param.10, f32[1024]{0:T(1024)S(1)} %copy-done.10, f32[384]{0:T(512)S(1)} %add_rsqrt_fusion, f32[384]{0:T(512)S(1)} %broadcast_multiply_fusion), kind=kOutput, calls=%fused_computation.47 | convolution fusion | flops 2417885184 | bytes 11803648 | tf_op jit(solution)/shard_map/dot_general | solution.py:99
  113.1 3.3 copy.21
  116.5 3.1 copy.25
  123.7 3.1 copy.22
  126.8 3.0 copy.26
  129.8 4.6 %add_convert_fusion = (bf16[384,1024]{1,0:T(8,128)(2,1)}, bf16[384,1024]{1,0:T(8,128)(2,1)S(1)}) fusion(f32[384,1024]{1,0:T(8,128)} %copy.26, f32[384,1024]{1,0:T(8,128)S(1)} %copy.20, f32[384,3072]{1,0:T(8,128)} %copy-done.1, f32[384,1024]{1,0:T(8,128)} %copy.22), kind=kLoop, calls=%fused_computation.44 | loop fusion | flops 2359296 | bytes 9437184 | tf_op jit(solution)/shard_map/convert_element_type | solution.py:40
  135.8 4.3 collective-permute-start
  140.1 3.0 collective-permute-start.1
  143.1 2.5 collective-permute-start.2
  145.6 4.3 collective-permute-start.3
  149.9 3.1 collective-permute-start.4
  153.0 138.8 %all_gather.14 = bf16[16,1024]{1,0:T(8,128)(2,1)} all-gather(bf16[16,256]{1,0:T(8,128)(2,1)S(1)} %copy-done.9), channel_id=1, replica_groups=mesh['tok'=64,'grp'=4] {'grp'}, dimensions={1}, use_global_device_ids=true | all-gather | bytes 40960 | tf_op jit(solution)/shard_map/all_gather | solution.py:96
  297.5 2.4 reshape.75
  299.9 4.8 %scatter_custom_fusion = bf16[192,8192]{1,0:T(8,128)(2,1)S(1)} fusion(s32[96]{0:T(128)} %fusion.46, bf16[96,8192]{1,0:T(8,128)(2,1)} %reshape.75, bf16[]{:T(256)} %constant.92.clone.1), kind=kCustom, calls=%fused_computation.42 | custom fusion | bytes 3146240 | tf_op jit(solution)/shard_map/scatter | solution.py:140
  304.7 4.4 all_to_all.8
  309.1 10.1 %all-to-all-start = ((bf16[64,3,8192]{2,1,0:T(4,128)(2,1)}), bf16[64,3,8192]{2,1,0:T(4,128)(2,1)}, u32[]{:S(2)}, u32[]{:S(2)}) async-start(bf16[64,3,8192]{2,1,0:T(4,128)(2,1)} %all_to_all.8), calls=%async_computation | async-start | bytes 8388608 | tf_op jit(solution)/shard_map/all_to_all | solution.py:141
  319.1 2.7 constant_dynamic-update-slice_fusion.6
  321.9 2.8 constant_dynamic-update-slice_fusion.5
  324.7 2.7 constant_dynamic-update-slice_fusion.4
  328.8 2.8 constant_dynamic-update-slice_fusion.2
  331.6 2.7 constant_dynamic-update-slice_fusion.1
  334.2 2.7 constant_dynamic-update-slice_fusion
  336.9 9.6 %fusion.47 = (bf16[1,2688,1024]{2,1,0:T(8,128)(2,1)}, bf16[1,2688,1024]{2,1,0:T(8,128)(2,1)}) fusion(bf16[2,2688,1024]{2,1,0:T(8,128)(2,1)} %constant_dynamic-update-slice_fusion), kind=kLoop, calls=%fused_computation.79 | loop fusion | bytes 22020096 | tf_op jit(solution)/shard_map/slice | solution.py:121
  346.5 8.0 %copy.28 = bf16[1,2688,1024]{1,2,0:T(8,128)(2,1)} copy(bf16[1,2688,1024]{2,1,0:T(8,128)(2,1)} %get-tuple-element.165) | data formatting | bytes 11010048 | tf_op jit(solution)/shard_map/slice | solution.py:121
  354.5 8.4 %copy.23 = bf16[1,2688,1024]{1,2,0:T(8,128)(2,1)} copy(bf16[1,2688,1024]{2,1,0:T(8,128)(2,1)} %get-tuple-element.166) | data formatting | bytes 11010048 | tf_op jit(solution)/shard_map/slice | solution.py:121
  362.9 78.1 %while.35 = (s32[]{:T(128)}, bf16[8,384,2,64]{1,3,2,0:T(8,128)(2,1)S(1)}, bf16[8,2688,2,64]{1,3,2,0:T(8,128)(2,1)}, bf16[8,384,2,64]{1,3,2,0:T(8,128)(2,1)}, bf1...) while((s32[]{:T(128)}, ...), condition=%wide.region_7.8_spmd.clone, body=%wide.region_4.7_spmd.clone.sunk | while | flops 552270336 | bytes 30602324 | solution.py:80
  363.6 3.2 fusion.59
  369.1 3.6 fusion.61
  373.3 3.2 fusion.59
  378.9 3.6 fusion.61
  383.1 3.2 fusion.59
  388.6 3.6 fusion.61
  392.9 3.2 fusion.59
  398.4 3.6 fusion.61
  402.6 3.2 fusion.59
  408.1 3.6 fusion.61
  412.4 3.2 fusion.59
  417.9 3.6 fusion.61
  422.1 3.2 fusion.59
  427.7 3.6 fusion.61
  431.9 3.2 fusion.59
  437.4 3.6 fusion.61
  441.0 3.5 convolution_convert_fusion
  444.5 7.4 %all_to_all.10 = bf16[192,8192]{1,0:T(8,128)(2,1)} reshape(bf16[64,3,8192]{2,1,0:T(4,128)(2,1)} %all-to-all-done) | data formatting | bytes 6291456 | tf_op jit(solution)/shard_map/all_to_all | solution.py:141
  (165 shorter events, 45.5 us)
Async XLA Ops:
  7.2 97.6 %all-gather.3.cloned.1.call-start = ((), (), s32[]{:S(2)}) async-start(), calls=%async_computation.1 | async-start | bytes 6389760 | tf_op jit(solution)/shard_map/all_gather | solution.py:101
  19.2 421.8 %all-gather.5.cloned.1.call-start = ((), (), s32[]{:S(2)}) async-start(), calls=%async_computation.2 | async-start | bytes 2129920 | tf_op jit(solution)/shard_map/all_gather | solution.py:125
  85.1 19.6 %copy-start.10 = (f32[1024]{0:T(1024)S(1)}, f32[1024]{0:T(1024)}, u32[]{:S(2)}) copy-start(f32[1024]{0:T(1024)} %param.11) | copy-start | bytes 12292
  109.9 3.2 copy-start.1
  113.1 21.3 %copy-start.4 = (bf16[1,384,1024]{2,1,0:T(8,128)(2,1)}, bf16[1,384,1024]{2,1,0:T(8,128)(2,1)S(1)}, u32[]{:S(2)}) copy-start(bf16[1,384,1024]{2,1,0:T(8,128)(2,1)S(1)} %slice_bitcast_fusion) | copy-start | bytes 2359300
  119.5 2.2 copy-start.8
  134.4 162.9 %copy-start.2 = (bf16[384,1024]{1,0:T(8,128)(2,1)}, bf16[384,1024]{1,0:T(8,128)(2,1)S(1)}, u32[]{:S(2)}) copy-start(bf16[384,1024]{1,0:T(8,128)(2,1)S(1)} %get-tuple-element.168) | copy-start | bytes 2359300
  134.4 18.6 %copy-start.9 = (bf16[16,256]{1,0:T(8,128)(2,1)S(1)}, bf16[16,256]{1,0:T(8,128)(2,1)}, u32[]{:S(2)}) copy-start(bf16[16,256]{1,0:T(8,128)(2,1)} %param.13) | copy-start | bytes 24580
  134.5 159.4 %copy-start = (s32[98304]{0:T(1024)S(1)}, s32[98304]{0:T(1024)}, u32[]{:S(2)}) copy-start(s32[98304]{0:T(1024)} %get-tuple-element.315) | copy-start | bytes 1179652
  134.5 159.5 %copy-start.11 = (s32[96,1]{0,1:T(1,128)S(1)}, s32[96,1]{0,1:T(1,128)}, u32[]{:S(2)}) copy-start(s32[96,1]{0,1:T(1,128)} %param.15) | copy-start | bytes 1156
  134.5 161.7 %copy-start.6 = (bf16[384,1024]{1,0:T(8,128)(2,1)S(1)}, bf16[384,1024]{1,0:T(8,128)(2,1)}, u32[]{:S(2)}) copy-start(bf16[384,1024]{1,0:T(8,128)(2,1)} %get-tuple-element.167) | copy-start | bytes 2359300
  135.8 156.1 %collective-permute-start = (bf16[2,384,1024]{2,1,0:T(8,128)(2,1)}, bf16[2,384,1024]{2,1,0:T(8,128)(2,1)}, u32[]{:S(2)}, u32[]{:S(2)}) collective-permute-start(bf16[2,384,1024]{2,1,0:T(8,128)(2,1)} %pad_maximum_fusion), channel_id=1, source_target_pairs={{0,3},{1,4},{2,5},{3,6},{4,7},{5,8},{6,9},{7,10},{8,11},{9,12},{10... | collective-permute-start | bytes 4718600 | tf_op jit(solution)/shard_map/ppermute | solution.py:17
  140.1 181.8 %collective-permute-start.1 = (bf16[2,384,1024]{2,1,0:T(8,128)(2,1)}, bf16[2,384,1024]{2,1,0:T(8,128)(2,1)}, u32[]{:S(2)}, u32[]{:S(2)}) collective-permute-start(bf16[2,384,1024]{2,1,0:T(8,128)(2,1)} %pad_maximum_fusion), channel_id=1, source_target_pairs={{0,2},{1,3},{2,4},{3,5},{4,6},{5,7},{6,8},{7,9},{8,10},{9,11},{10,... | collective-permute-start | bytes 4718600 | tf_op jit(solution)/shard_map/ppermute | solution.py:17
  143.1 181.6 %collective-permute-start.2 = (bf16[2,384,1024]{2,1,0:T(8,128)(2,1)}, bf16[2,384,1024]{2,1,0:T(8,128)(2,1)}, u32[]{:S(2)}, u32[]{:S(2)}) collective-permute-start(bf16[2,384,1024]{2,1,0:T(8,128)(2,1)} %pad_maximum_fusion), channel_id=1, source_target_pairs={{0,1},{1,2},{2,3},{3,4},{4,5},{5,6},{6,7},{7,8},{8,9},{9,10},{10,1... | collective-permute-start | bytes 4718600 | tf_op jit(solution)/shard_map/ppermute | solution.py:17
  145.6 183.2 %collective-permute-start.3 = (bf16[2,384,1024]{2,1,0:T(8,128)(2,1)}, bf16[2,384,1024]{2,1,0:T(8,128)(2,1)}, u32[]{:S(2)}, u32[]{:S(2)}) collective-permute-start(bf16[2,384,1024]{2,1,0:T(8,128)(2,1)} %pad_maximum_fusion), channel_id=1, source_target_pairs={{1,0},{2,1},{3,2},{4,3},{5,4},{6,5},{7,6},{8,7},{9,8},{10,9},{11,1... | collective-permute-start | bytes 4718600 | tf_op jit(solution)/shard_map/ppermute | solution.py:17
  149.9 181.7 %collective-permute-start.4 = (bf16[2,384,1024]{2,1,0:T(8,128)(2,1)}, bf16[2,384,1024]{2,1,0:T(8,128)(2,1)}, u32[]{:S(2)}, u32[]{:S(2)}) collective-permute-start(bf16[2,384,1024]{2,1,0:T(8,128)(2,1)} %pad_maximum_fusion), channel_id=1, source_target_pairs={{2,0},{3,1},{4,2},{5,3},{6,4},{7,5},{8,6},{9,7},{10,8},{11,9},{12,... | collective-permute-start | bytes 4718600 | tf_op jit(solution)/shard_map/ppermute | solution.py:17
  291.9 42.4 %collective-permute-start.5 = (bf16[2,384,1024]{2,1,0:T(8,128)(2,1)}, bf16[2,384,1024]{2,1,0:T(8,128)(2,1)}, u32[]{:S(2)}, u32[]{:S(2)}) collective-permute-start(bf16[2,384,1024]{2,1,0:T(8,128)(2,1)} %pad_maximum_fusion), channel_id=1, source_target_pairs={{3,0},{4,1},{5,2},{6,3},{7,4},{8,5},{9,6},{10,7},{11,8},{12,9},{13... | collective-permute-start | bytes 4718600 | tf_op jit(solution)/shard_map/ppermute | solution.py:17
  309.1 135.4 %all-to-all-start = ((bf16[64,3,8192]{2,1,0:T(4,128)(2,1)}), bf16[64,3,8192]{2,1,0:T(4,128)(2,1)}, u32[]{:S(2)}, u32[]{:S(2)}) async-start(bf16[64,3,8192]{2,1,0:T(4,128)(2,1)} %all_to_all.8), calls=%async_computation | async-start | bytes 8388608 | tf_op jit(solution)/shard_map/all_to_all | solution.py:141
  321.9 5.5 %copy-start.3 = (bf16[384,1024]{1,0:T(8,128)(2,1)S(1)}, bf16[384,1024]{1,0:T(8,128)(2,1)}, u32[]{:S(2)}) copy-start(bf16[384,1024]{1,0:T(8,128)(2,1)} %copy-done.2) | copy-start | bytes 2359300
  321.9 5.5 %copy-start.5 = (bf16[1,384,1024]{2,1,0:T(8,128)(2,1)S(1)}, bf16[1,384,1024]{2,1,0:T(8,128)(2,1)}, u32[]{:S(2)}) copy-start(bf16[1,384,1024]{2,1,0:T(8,128)(2,1)} %copy-done.4) | copy-start | bytes 2359300
  354.5 8.4 %copy-start.7 = (bf16[8,384,2,64]{1,3,2,0:T(8,128)(2,1)S(1)}, bf16[8,384,2,64]{1,3,2,0:T(8,128)(2,1)}, u32[]{:S(2)}) copy-start(bf16[8,384,2,64]{1,3,2,0:T(8,128)(2,1)} %custom-call.5) | copy-start | bytes 2359300
Sparse Core Ops, SparseCore 0:
  19.3 85.4 all-gather.2
  292.0 87.7 all-gather.4
where the time goes:
time: 461 us; the launch traced here: 459 us
  blocking collectives  151 us (33%)
  local copies, waits for them, and re-layouts  144 us (31%)
  matrix products  62.8 us (14%)
  other arithmetic  40.6 us (9%)
  starting transfers between devices  29.3 us (6%)
  waiting for transfers between devices  16.1 us (3%)
  between operations  14.3 us (3%)
    all_gather x1, blocking collectives, per_device(): lax.all_gather(output_weight, 'grp', axis=1, tiled=True)  139 us
    gather x17, local copies, waits for them, and re-layouts, positions_of(): starts = jnp.searchsorted(segment_ids, own_ids, side='left')  62.7 us
    dot_general x8, matrix products, one_pair(): jnp.einsum('nts,snd->tnd', weights, value_pair, preferred_element_type=jn...  28.5 us
    slice x3, local copies, waits for them, and re-layouts, per_device(): mixed_rows = attend_pairs(queries, window[0], window[1], allowed, H)  26 us
    dot_general x8, matrix products, pair_scores(): jnp.einsum('tnd,snd->nts', query_pair, key_pair, preferred_element_type=j...  25.7 us
    ppermute x6, starting transfers between devices, shifted(): lax.ppermute(value, axis, [(source, source + steps) for source in range(i...  19.1 us
    reduce_sum x8, other arithmetic, one_pair(): row_total = jnp.sum(exponent, axis=-1)  18.5 us
    all_gather x1, waiting for transfers between devices, per_device(): lax.all_gather(input_cols, 'tok', axis=0, tiled=True)  16 us
  transfers between devices with their start and end apart: 9, of which 1 were waited for; matrix products, arithmetic and copies ran while one was open for 45% of the time, Pallas kernels for 0%

commit v1 on v0

--- a/solution.py
+++ b/solution.py
@@ -98,7 +98,9 @@
     section = normed
     joined = jnp.dot(
         section,
-        lax.all_gather(input_cols, "tok", axis=0, tiled=True),
+        jnp.concatenate(
+            lax.all_to_all(jnp.stack([input_cols] * lax.axis_size("tok")), "tok", 0, 0), axis=0
+        ),
         preferred_element_type=jnp.float32,
     )
     own_ids = lax.dynamic_slice_in_dim(segment_ids, first_row, row_count, 0)

time: 461 us -> 530 us (1.15)
  waiting for transfers between devices: 16.1 us -> 91.6 us
  local copies, waits for them, and re-layouts: 144 us -> 126 us
  starting transfers between devices: 29.3 us -> 43.6 us
    all_to_all x0 -> x1, waiting for transfers between devices: none -> 91.5 us  [per_device(): lax.all_to_all(jnp.stack([input_cols] * lax.axis_size('tok')), 'tok', 0, 0)]
    gather x17, local copies, waits for them, and re-layouts: 62.7 us -> 43.1 us  [positions_of(): starts = jnp.searchsorted(segment_ids, own_ids, side='left')]
    all_gather x1 -> x0, waiting for transfers between devices: 16 us -> none  [per_device(): lax.all_gather(input_cols, 'tok', axis=0, tiled=True)]
    all_to_all x0 -> x1, starting transfers between devices: none -> 15.5 us  [per_device(): lax.all_to_all(jnp.stack([input_cols] * lax.axis_size('tok')), 'tok', 0, 0)]
    unnamed x29 -> x27, local copies, waits for them, and re-layouts: 14.6 us -> 14.6 us
  transfers between devices with their start and end apart: 9 -> 9, of which waited for: 1 -> 1; matrix products, arithmetic and copies ran while one was open for 45% -> 35% of each run, Pallas kernels for 0% -> 0%
where the time goes in v1:
time: 530 us; the launch traced here: 528 us
  blocking collectives  149 us (28%)
  local copies, waits for them, and re-layouts  126 us (24%)
  waiting for transfers between devices  91.6 us (17%)
  matrix products  62.8 us (12%)
  starting transfers between devices  43.6 us (8%)
  other arithmetic  39.9 us (8%)
  between operations  14.3 us (3%)
    all_gather x1, blocking collectives, per_device(): lax.all_gather(output_weight, 'grp', axis=1, tiled=True)  138 us
    all_to_all x1, waiting for transfers between devices, per_device(): lax.all_to_all(jnp.stack([input_cols] * lax.axis_size('tok')), 'tok', 0, 0)  91.5 us
    gather x17, local copies, waits for them, and re-layouts, positions_of(): starts = jnp.searchsorted(segment_ids, own_ids, side='left')  43.1 us
    dot_general x8, matrix products, one_pair(): jnp.einsum('nts,snd->tnd', weights, value_pair, preferred_element_type=jn...  28.5 us
    dot_general x8, matrix products, pair_scores(): jnp.einsum('tnd,snd->nts', query_pair, key_pair, preferred_element_type=j...  25.6 us
    slice x3, local copies, waits for them, and re-layouts, per_device(): mixed_rows = attend_pairs(queries, window[0], window[1], allowed, H)  25.5 us
    ppermute x6, starting transfers between devices, shifted(): lax.ppermute(value, axis, [(source, source + steps) for source in range(i...  19 us
    reduce_sum x8, other arithmetic, one_pair(): row_total = jnp.sum(exponent, axis=-1)  18.5 us
  transfers between devices with their start and end apart: 9, of which 1 were waited for; matrix products, arithmetic and copies ran while one was open for 35% of the time, Pallas kernels for 0%

profile of v1, /device:TPU:1, one launch (start us, length us, event | category | flops | bytes accessed | tf_op | source)
XLA Modules:
  0.0 528.5 jit_solution(6284467351711148417)
XLA Ops:
  7.2 10.4 %all_gather.9 = bf16[16,3072]{1,0:T(8,128)(2,1)S(1)} all-gather(bf16[16,768]{1,0:T(8,128)(2,1)} %param.12), channel_id=1, replica_groups=mesh['tok'=64,'grp'=4] {'grp'}, dimensions={1}, use_global_device_ids=true | all-gather | bytes 122880 | tf_op jit(solution)/shard_map/all_gather | solution.py:95
  17.6 3.4 stack.8
  21.0 15.5 %all-to-all-start = ((bf16[64,16,3072]{2,1,0:T(8,128)(2,1)}), bf16[64,16,3072]{2,1,0:T(8,128)(2,1)}, u32[]{:S(2)}, u32[]{:S(2)}) async-start(bf16[64,16,3072]{2,1,0:T(8,128)(2,1)} %stack.8), calls=%async_computation | async-start | bytes 12582912 | tf_op jit(solution)/shard_map/all_to_all | solution.py:102
  36.7 44.7 %while.36 = (s32[]{:T(128)}, u32[384]{0:T(512)S(1)}, u32[384]{0:T(512)S(1)}, s32[98304]{0:T(1024)S(1)}, s32[384]{0:T(512)S(1)}, /*index=5*/s32[]{:T(128)}, s32[]{:T(128)}, s32[]{}) while((s32[]{:T(128)}, u32[384]{0:T(512)S(1)}, u32[384]{0:T(512)S(1)}, s32[98304]{0:T(1024)S(1)}, s32[384]{0:T(512)S(1)}, /*index=5*/s32[]{:T(128)}, ...), condition=%wide.region_3.4_spmd.clone, body=%wide.region_2.3_spmd.clone.sunk | while | flops 7940 | bytes 31085 | solution.py:45
  36.7 2.5 gather_fusion
  39.3 2.5 gather_fusion
  42.0 2.5 gather_fusion
  44.6 2.5 gather_fusion
  47.2 2.5 gather_fusion
  49.9 2.5 gather_fusion
  52.5 2.5 gather_fusion
  55.1 2.5 gather_fusion
  57.8 2.5 gather_fusion
  60.4 2.5 gather_fusion
  63.0 2.5 gather_fusion
  65.7 2.5 gather_fusion
  68.3 2.5 gather_fusion
  70.9 2.5 gather_fusion
  73.6 2.5 gather_fusion
  76.2 2.5 gather_fusion
  78.8 2.5 gather_fusion
  85.8 91.5 %all-to-all-done = bf16[64,16,3072]{2,1,0:T(8,128)(2,1)} async-done(((bf16[64,16,3072]{2,1,0:T(8,128)(2,1)}), bf16[64,16,3072]{2,1,0:T(8,128)(2,1)}, u32[]{:S(2)}, u32[]{:S(2)}) %all-to-all-start) | async-done | bytes 6291488 | tf_op jit(solution)/shard_map/all_to_all | solution.py:102
  177.3 5.1 fusion.38
  185.7 3.3 copy.21
  189.1 3.1 copy.25
  196.3 3.1 copy.22
  199.4 3.0 copy.26
  202.5 4.6 add_convert_fusion
  208.4 4.0 collective-permute-start
  214.4 2.5 collective-permute-start.2
  216.9 4.3 collective-permute-start.3
  221.2 4.2 collective-permute-start.4
  225.4 138.1 %all_gather.10 = bf16[16,1024]{1,0:T(8,128)(2,1)} all-gather(bf16[16,256]{1,0:T(8,128)(2,1)S(1)} %copy-done.9), channel_id=1, replica_groups=mesh['tok'=64,'grp'=4] {'grp'}, dimensions={1}, use_global_device_ids=true | all-gather | bytes 40960 | tf_op jit(solution)/shard_map/all_gather | solution.py:96
  371.3 4.6 scatter_custom_fusion
  375.9 4.4 all_to_all.12
  380.3 9.0 %all-to-all-start.1 = ((bf16[64,3,8192]{2,1,0:T(4,128)(2,1)}), bf16[64,3,8192]{2,1,0:T(4,128)(2,1)}, u32[]{:S(2)}, u32[]{:S(2)}) async-start(bf16[64,3,8192]{2,1,0:T(4,128)(2,1)} %all_to_all.12), calls=%async_computation.1 | async-start | bytes 8388608 | tf_op jit(solution)/shard_map/all_to_all | solution.py:143
  389.3 2.7 constant_dynamic-update-slice_fusion.6
  392.1 2.9 constant_dynamic-update-slice_fusion.5
  394.9 2.7 constant_dynamic-update-slice_fusion.4
  399.0 2.8 constant_dynamic-update-slice_fusion.2
  401.8 2.6 constant_dynamic-update-slice_fusion.1
  404.4 2.7 constant_dynamic-update-slice_fusion
  407.1 9.6 %fusion.47 = (bf16[1,2688,1024]{2,1,0:T(8,128)(2,1)}, bf16[1,2688,1024]{2,1,0:T(8,128)(2,1)}) fusion(bf16[2,2688,1024]{2,1,0:T(8,128)(2,1)} %constant_dynamic-update-slice_fusion), kind=kLoop, calls=%fused_computation.79 | loop fusion | bytes 22020096 | tf_op jit(solution)/shard_map/slice | solution.py:123
  416.7 7.9 %copy.28 = bf16[1,2688,1024]{1,2,0:T(8,128)(2,1)} copy(bf16[1,2688,1024]{2,1,0:T(8,128)(2,1)} %get-tuple-element.165) | data formatting | bytes 11010048 | tf_op jit(solution)/shard_map/slice | solution.py:123
  424.6 8.0 %copy.23 = bf16[1,2688,1024]{1,2,0:T(8,128)(2,1)} copy(bf16[1,2688,1024]{2,1,0:T(8,128)(2,1)} %get-tuple-element.166) | data formatting | bytes 11010048 | tf_op jit(solution)/shard_map/slice | solution.py:123
  432.6 78.1 %while.35 = (s32[]{:T(128)}, bf16[8,384,2,64]{1,3,2,0:T(8,128)(2,1)S(1)}, bf16[8,2688,2,64]{1,3,2,0:T(8,128)(2,1)}, bf16[8,384,2,64]{1,3,2,0:T(8,128)(2,1)}, bf1...) while((s32[]{:T(128)}, ...), condition=%wide.region_7.8_spmd.clone, body=%wide.region_4.7_spmd.clone.sunk | while | flops 552270336 | bytes 30602324 | solution.py:80
  433.3 3.2 fusion.59
  438.8 3.6 fusion.61
  443.0 3.2 fusion.59
  448.5 3.6 fusion.61
  452.8 3.2 fusion.59
  458.3 3.6 fusion.61
  462.5 3.2 fusion.59
  468.1 3.6 fusion.61
  472.3 3.2 fusion.59
  477.8 3.6 fusion.61
  482.1 3.2 fusion.59
  487.6 3.6 fusion.61
  491.8 3.2 fusion.59
  497.3 3.6 fusion.61
  501.6 3.2 fusion.59
  507.1 3.6 fusion.61
  510.7 3.5 convolution_convert_fusion
  514.2 7.4 %all_to_all.14 = bf16[192,8192]{1,0:T(8,128)(2,1)} reshape(bf16[64,3,8192]{2,1,0:T(4,128)(2,1)} %all-to-all-done.1) | data formatting | bytes 6291456 | tf_op jit(solution)/shard_map/all_to_all | solution.py:143
  (163 shorter events, 48.6 us)
Async XLA Ops:
  21.0 15.6 %copy-start = (s32[98304]{0:T(1024)S(1)}, s32[98304]{0:T(1024)}, u32[]{:S(2)}) copy-start(s32[98304]{0:T(1024)} %param.14) | copy-start | bytes 1179652
  21.0 156.3 %all-to-all-start = ((bf16[64,16,3072]{2,1,0:T(8,128)(2,1)}), bf16[64,16,3072]{2,1,0:T(8,128)(2,1)}, u32[]{:S(2)}, u32[]{:S(2)}) async-start(bf16[64,16,3072]{2,1,0:T(8,128)(2,1)} %stack.8), calls=%async_computation | async-start | bytes 12582912 | tf_op jit(solution)/shard_map/all_to_all | solution.py:102
  36.5 474.2 %all-gather.2.cloned.1.call-start = ((), (), s32[]{:S(2)}) async-start(), calls=%async_computation.2 | async-start | bytes 2129920 | tf_op jit(solution)/shard_map/all_gather | solution.py:127
  182.5 3.1 copy-start.1
  185.7 21.4 %copy-start.4 = (bf16[1,384,1024]{2,1,0:T(8,128)(2,1)}, bf16[1,384,1024]{2,1,0:T(8,128)(2,1)S(1)}, u32[]{:S(2)}) copy-start(bf16[1,384,1024]{2,1,0:T(8,128)(2,1)S(1)} %slice_bitcast_fusion) | copy-start | bytes 2359300
  192.1 2.2 copy-start.8
  207.1 161.6 %copy-start.2 = (bf16[384,1024]{1,0:T(8,128)(2,1)}, bf16[384,1024]{1,0:T(8,128)(2,1)S(1)}, u32[]{:S(2)}) copy-start(bf16[384,1024]{1,0:T(8,128)(2,1)S(1)} %get-tuple-element.168) | copy-start | bytes 2359300
  207.1 18.3 %copy-start.9 = (bf16[16,256]{1,0:T(8,128)(2,1)S(1)}, bf16[16,256]{1,0:T(8,128)(2,1)}, u32[]{:S(2)}) copy-start(bf16[16,256]{1,0:T(8,128)(2,1)} %param.13) | copy-start | bytes 24580
  207.1 158.7 %copy-start.10 = (s32[96,1]{0,1:T(1,128)S(1)}, s32[96,1]{0,1:T(1,128)}, u32[]{:S(2)}) copy-start(s32[96,1]{0,1:T(1,128)} %param.15) | copy-start | bytes 1156
  207.1 160.4 %copy-start.6 = (bf16[384,1024]{1,0:T(8,128)(2,1)S(1)}, bf16[384,1024]{1,0:T(8,128)(2,1)}, u32[]{:S(2)}) copy-start(bf16[384,1024]{1,0:T(8,128)(2,1)} %get-tuple-element.167) | copy-start | bytes 2359300
  208.4 155.2 %collective-permute-start = (bf16[2,384,1024]{2,1,0:T(8,128)(2,1)}, bf16[2,384,1024]{2,1,0:T(8,128)(2,1)}, u32[]{:S(2)}, u32[]{:S(2)}) collective-permute-start(bf16[2,384,1024]{2,1,0:T(8,128)(2,1)} %pad_maximum_fusion), channel_id=1, source_target_pairs={{0,3},{1,4},{2,5},{3,6},{4,7},{5,8},{6,9},{7,10},{8,11},{9,12},{10... | collective-permute-start | bytes 4718600 | tf_op jit(solution)/shard_map/ppermute | solution.py:17
  212.4 179.6 %collective-permute-start.1 = (bf16[2,384,1024]{2,1,0:T(8,128)(2,1)}, bf16[2,384,1024]{2,1,0:T(8,128)(2,1)}, u32[]{:S(2)}, u32[]{:S(2)}) collective-permute-start(bf16[2,384,1024]{2,1,0:T(8,128)(2,1)} %pad_maximum_fusion), channel_id=1, source_target_pairs={{0,2},{1,3},{2,4},{3,5},{4,6},{5,7},{6,8},{7,9},{8,10},{9,11},{10,... | collective-permute-start | bytes 4718600 | tf_op jit(solution)/shard_map/ppermute | solution.py:17
  214.4 180.5 %collective-permute-start.2 = (bf16[2,384,1024]{2,1,0:T(8,128)(2,1)}, bf16[2,384,1024]{2,1,0:T(8,128)(2,1)}, u32[]{:S(2)}, u32[]{:S(2)}) collective-permute-start(bf16[2,384,1024]{2,1,0:T(8,128)(2,1)} %pad_maximum_fusion), channel_id=1, source_target_pairs={{0,1},{1,2},{2,3},{3,4},{4,5},{5,6},{6,7},{7,8},{8,9},{9,10},{10,1... | collective-permute-start | bytes 4718600 | tf_op jit(solution)/shard_map/ppermute | solution.py:17
  216.9 182.1 %collective-permute-start.3 = (bf16[2,384,1024]{2,1,0:T(8,128)(2,1)}, bf16[2,384,1024]{2,1,0:T(8,128)(2,1)}, u32[]{:S(2)}, u32[]{:S(2)}) collective-permute-start(bf16[2,384,1024]{2,1,0:T(8,128)(2,1)} %pad_maximum_fusion), channel_id=1, source_target_pairs={{1,0},{2,1},{3,2},{4,3},{5,4},{6,5},{7,6},{8,7},{9,8},{10,9},{11,1... | collective-permute-start | bytes 4718600 | tf_op jit(solution)/shard_map/ppermute | solution.py:17
  221.2 180.6 %collective-permute-start.4 = (bf16[2,384,1024]{2,1,0:T(8,128)(2,1)}, bf16[2,384,1024]{2,1,0:T(8,128)(2,1)}, u32[]{:S(2)}, u32[]{:S(2)}) collective-permute-start(bf16[2,384,1024]{2,1,0:T(8,128)(2,1)} %pad_maximum_fusion), channel_id=1, source_target_pairs={{2,0},{3,1},{4,2},{5,3},{6,4},{7,5},{8,6},{9,7},{10,8},{11,9},{12,... | collective-permute-start | bytes 4718600 | tf_op jit(solution)/shard_map/ppermute | solution.py:17
  363.6 40.8 %collective-permute-start.5 = (bf16[2,384,1024]{2,1,0:T(8,128)(2,1)}, bf16[2,384,1024]{2,1,0:T(8,128)(2,1)}, u32[]{:S(2)}, u32[]{:S(2)}) collective-permute-start(bf16[2,384,1024]{2,1,0:T(8,128)(2,1)} %pad_maximum_fusion), channel_id=1, source_target_pairs={{3,0},{4,1},{5,2},{6,3},{7,4},{8,5},{9,6},{10,7},{11,8},{12,9},{13... | collective-permute-start | bytes 4718600 | tf_op jit(solution)/shard_map/ppermute | solution.py:17
  380.3 133.9 %all-to-all-start.1 = ((bf16[64,3,8192]{2,1,0:T(4,128)(2,1)}), bf16[64,3,8192]{2,1,0:T(4,128)(2,1)}, u32[]{:S(2)}, u32[]{:S(2)}) async-start(bf16[64,3,8192]{2,1,0:T(4,128)(2,1)} %all_to_all.12), calls=%async_computation.1 | async-start | bytes 8388608 | tf_op jit(solution)/shard_map/all_to_all | solution.py:143
  392.0 5.6 %copy-start.3 = (bf16[384,1024]{1,0:T(8,128)(2,1)S(1)}, bf16[384,1024]{1,0:T(8,128)(2,1)}, u32[]{:S(2)}) copy-start(bf16[384,1024]{1,0:T(8,128)(2,1)} %copy-done.2) | copy-start | bytes 2359300
  392.0 5.6 %copy-start.5 = (bf16[1,384,1024]{2,1,0:T(8,128)(2,1)S(1)}, bf16[1,384,1024]{2,1,0:T(8,128)(2,1)}, u32[]{:S(2)}) copy-start(bf16[1,384,1024]{2,1,0:T(8,128)(2,1)} %copy-done.4) | copy-start | bytes 2359300
  424.6 8.0 %copy-start.7 = (bf16[8,384,2,64]{1,3,2,0:T(8,128)(2,1)S(1)}, bf16[8,384,2,64]{1,3,2,0:T(8,128)(2,1)}, u32[]{:S(2)}) copy-start(bf16[8,384,2,64]{1,3,2,0:T(8,128)(2,1)} %custom-call.5) | copy-start | bytes 2359300
Sparse Core Ops, SparseCore 0:
  363.7 86.6 all-gather.1
